TPU v7x, 128 devices: a whole 4x4x4 slice. The times are simulated.
128 devices in a mesh: row: 16 (over z, y_hi, core), col: 8 (over y_lo, x).
Axes of the slice: x: 4, y: 4 (y_hi: 2, y_lo: 2; y = y_hi * 2 + y_lo), z: 4, core: 2. Of those that a mesh axis runs over, the one named last changes fastest.
Arguments:
- sky_image: bfloat16 [2, 16384, 16384], P(None, 'row', 'col'), may hold values from -6 to 6
- facet_rows: int32 [128], replicated, may hold values from 512 to 15872
- facet_offsets: int32 [128], replicated, may hold values from 0 to 127
- facet_owner: int32 [128], replicated, may hold values from 0 to 127, each once
Outputs:
- facets: bfloat16 [128, 2, 1024, 1024], P(('row', 'col'))
Inputs may be any that keep to these rules, and one draw needn't show every extreme that they name: `facet_owner`: the entries are distinct, so every device owns exactly one facet.
All inputs are finite; a program needn't handle non-finite values.
Results may differ from a plain program's by a relative error of at most 0.0095.
Values may be sent and summed in bfloat16 or wider, within the bound.
No kernel may reach another device: no remote copies, remote signals or barrier semaphores. Data moves between devices by JAX's collectives and lax.ppermute only.
A program may use at most 128 MiB of HBM per device.

v0:
```python
import math
import jax
import jax.numpy as jnp
from jax import lax
from jax.sharding import PartitionSpec as P

N = 16384
FS = 1024
SPLIT = 128


def split_up(shard, dim, devices):
    lengths = shard.shape
    parts = shard.reshape(*lengths[:dim], devices, lengths[dim] // devices, *lengths[dim + 1 :])
    return jnp.moveaxis(parts, dim, 0)


def edges_of(length, count):
    unit = 8 if length >= 8 * count else 1
    return [length // unit * k // count * unit for k in range(1, count)]


def joined_along(parts, dim):
    lengths = list(parts.shape[1:])
    lengths[dim] *= parts.shape[0]
    return jnp.moveaxis(parts, 0, dim).reshape(lengths)


def cut_exchange(shard, axis, pieces, split_dim, concat_dim):
    parts = split_up(shard, split_dim, lax.axis_size(axis))
    widest = max(range(1, max(2, parts.ndim - 1)), key=lambda d: parts.shape[d])
    gathered = []
    for share in jnp.split(parts, edges_of(parts.shape[widest], pieces), axis=widest):
        if share.size:
            gathered.append(lax.all_to_all(share, axis, split_axis=0, concat_axis=0, tiled=True))
    return joined_along(jnp.concatenate(gathered, axis=widest), concat_dim)


def shifted(block, axis, distance):
    devices = range(lax.axis_size(axis))
    route = [((i - distance) % len(devices), i) for i in devices]
    return lax.ppermute(block, axis, route)


def dft_table(length):
    positions = jnp.arange(length, dtype=jnp.int32)
    turn_count = positions[:, None] * positions[None, :] % length
    angles = turn_count.astype(jnp.float32) * (-2.0 * math.pi / length)
    factor = 1.0 / math.sqrt(length)
    return (
        (jnp.cos(angles) * factor).astype(jnp.bfloat16),
        (jnp.sin(angles) * factor).astype(jnp.bfloat16),
    )


def twiddle_table(first_len, second_len, total):
    left_index = jnp.arange(first_len, dtype=jnp.int32)[:, None]
    right_index = jnp.arange(second_len, dtype=jnp.int32)[None, :]
    angles = (left_index * right_index % total).astype(jnp.float32) * (-2.0 * math.pi / total)
    return (jnp.cos(angles), jnp.sin(angles))


def complex_mix(formula, tables, values):
    re_part = jnp.einsum(
        formula, tables[0], values[0], preferred_element_type=jnp.float32
    ) - jnp.einsum(formula, tables[1], values[1], preferred_element_type=jnp.float32)
    im_part = jnp.einsum(
        formula, tables[0], values[1], preferred_element_type=jnp.float32
    ) + jnp.einsum(formula, tables[1], values[0], preferred_element_type=jnp.float32)
    return (re_part, im_part)


def rotate(pair, twiddle):
    return (
        pair[0] * twiddle[0] - pair[1] * twiddle[1],
        pair[0] * twiddle[1] + pair[1] * twiddle[0],
    )


def as_stored(pair):
    return jnp.stack((pair[0].astype(jnp.bfloat16), pair[1].astype(jnp.bfloat16)))


def rows_pass(strip_rows):
    row_count = strip_rows.shape[1]
    lead_len = N // SPLIT
    blocks = strip_rows.reshape(2, row_count, lead_len, SPLIT)
    mixed_pair = complex_mix("pa,rab->rpb", dft_table(lead_len), (blocks[0], blocks[1]))
    section_one = as_stored(rotate(mixed_pair, twiddle_table(lead_len, SPLIT, N)))
    mixed_pair = complex_mix("qb,rpb->rqp", dft_table(SPLIT), (section_one[0], section_one[1]))
    return as_stored(mixed_pair).reshape(2, row_count, N)


def shards(sky_image, facet_rows, facet_offsets, facet_owner):
    strip_rows = lax.all_to_all(sky_image, "col", split_axis=1, concat_axis=2, tiled=True)
    rows_done = rows_pass(strip_rows)
    row_devices = lax.axis_size("row")
    col_devices = lax.axis_size("col")
    devices = row_devices * col_devices
    strip_len = rows_done.shape[1]
    tables = dft_table(devices)
    twiddle = twiddle_table(devices, strip_len, N)
    twiddle = (twiddle[0][:, :, None], twiddle[1][:, :, None])
    columns = cut_exchange(rows_done, ("row", "col"), 2, 2, 1)
    col_width = columns.shape[2]
    grouped = columns.reshape(2, devices, strip_len, col_width)
    mixed_pair = complex_mix("pg,gic->pic", tables, (grouped[0], grouped[1]))
    section_two = as_stored(rotate(mixed_pair, twiddle))
    mixed_pair = complex_mix("qi,pic->qpc", dft_table(strip_len), (section_two[0], section_two[1]))
    grid_cols = as_stored(mixed_pair).reshape(2, N, col_width)
    my_index = lax.axis_index(("row", "col"))
    device_ids = jnp.arange(devices, dtype=jnp.int32)
    matches = (facet_owner[None, :] == device_ids[:, None]).astype(jnp.int32)
    owned_count = jnp.sum(matches, axis=1)
    centre_row = jnp.where(owned_count > 0, jnp.sum(matches * facet_rows[None, :], axis=1), FS // 2)
    centre_col = jnp.sum(matches * facet_offsets[None, :], axis=1)
    reach_blocks = FS // (2 * col_width)
    pieces = []
    for distance in range(reach_blocks, -reach_blocks - 1, -1):
        target = (my_index + distance) % devices
        start_row = centre_row[target] - FS // 2
        band_rows = lax.dynamic_slice_in_dim(grid_cols, start_row, FS, 1)
        if distance != 0:
            band_rows = shifted(band_rows, ("row", "col"), distance)
        pieces.append(band_rows)
    window = jnp.concatenate(pieces, axis=2)
    facet_tile = lax.dynamic_slice_in_dim(window, centre_col[my_index], FS, 2)
    taper_axis = 0.25 + 0.75 * jnp.sin(math.pi * (jnp.arange(FS, dtype=jnp.float32) + 0.5) / FS)
    weight = taper_axis[:, None] * taper_axis[None, :] * owned_count[my_index].astype(jnp.float32)
    return (facet_tile.astype(jnp.float32) * weight).astype(jnp.bfloat16)[None]


def solution(mesh):
    placed = (P(None, "row", "col"), P(), P(), P())
    return jax.shard_map(
        shards,
        mesh=mesh,
        in_specs=placed,
        out_specs=P(("row", "col"), None, None, None),
        check_vma=False,
    )
```

profile of v0, /device:TPU:21, one launch (start us, length us, event | category | flops | bytes accessed | tf_op | source)
XLA Modules:
  0.0 524.7 jit_solution(18393274846443005914)
XLA Ops:
  0.0 16.4 %copy.29 = bf16[2,1024,2048]{2,0,1:T(2,128)(2,1)} copy(bf16[2,1024,2048]{2,1,0:T(8,128)(2,1)} %param.4) | data formatting | bytes 16777216 | tf_op args[0]
  16.4 5.1 all-to-all-start
  21.8 114.8 %all-to-all-done = bf16[2,1024,2048]{2,0,1:T(2,128)(2,1)} async-done(((bf16[2,1024,2048]{2,0,1:T(2,128)(2,1)}), bf16[2,1024,2048]{2,0,1:T(2,128)(2,1)}, u32[]{:S(2)}, u32[]{:S(2)}) %all-to-all-start) | async-done | bytes 8388640 | tf_op jit(solution)/shard_map/all_to_all | solution.py:95
  136.5 11.2 %copy.56 = bf16[2,8,128,2048]{3,1,2,0:T(8,128)(2,1)} copy(bf16[2,8,128,2048]{3,0,2,1:T(2,128)(2,1)} %bitcast.1) | data formatting | bytes 16777216 | tf_op jit(solution)/shard_map/all_to_all | solution.py:95
  147.7 6.1 %fusion.149 = (bf16[1,128,8,2048]{3,2,1,0:T(8,128)(2,1)}, bf16[1,128,8,2048]{3,2,1,0:T(8,128)(2,1)}) fusion(bf16[2,128,8,2048]{3,2,1,0:T(8,128)(2,1)} %bitcast.94), kind=kLoop, calls=%fused_computation.184 | loop fusion | bytes 16777216 | tf_op jit(solution)/shard_map/slice | solution.py:88
  153.9 7.4 %squeeze.11 = bf16[128,128,128]{2,1,0:T(8,128)(2,1)} reshape(bf16[1,128,8,2048]{3,2,1,0:T(8,128)(2,1)} %get-tuple-element.24) | data formatting | bytes 8388608 | tf_op jit(solution)/shard_map/squeeze | solution.py:88
  161.3 7.1 %fusion.54 = f32[128,128,128]{2,0,1:T(8,128)} fusion(bf16[128,128,128]{2,1,0:T(8,128)(2,1)} %squeeze.11), kind=kOutput, calls=%fused_computation.88 | convolution fusion | flops 537133056 | bytes 12582912 | tf_op jit(solution)/shard_map/pa,rab->rpb/dot_general | solution.py:66
  168.3 4.7 fusion.64
  173.0 7.4 %squeeze.10 = bf16[128,128,128]{2,1,0:T(8,128)(2,1)} reshape(bf16[1,128,8,2048]{3,2,1,0:T(8,128)(2,1)} %get-tuple-element.23) | data formatting | bytes 8388608 | tf_op jit(solution)/shard_map/squeeze | solution.py:88
  180.4 7.1 %fusion.52 = f32[128,128,128]{2,0,1:T(8,128)} fusion(bf16[128,128,128]{2,1,0:T(8,128)(2,1)} %squeeze.10), kind=kOutput, calls=%fused_computation.87 | convolution fusion | flops 537133056 | bytes 12582912 | tf_op jit(solution)/shard_map/pa,rab->rpb/dot_general | solution.py:69
  187.5 10.6 %fusion = (bf16[128,128,128]{2,1,0:T(8,128)(2,1)S(1)}, bf16[128,128,128]{2,1,0:T(8,128)(2,1)S(1)}) fusion(f32[128,128]{1,0:T(8,128)S(1)} %get-tuple-element.34, f32[128,128]{1,0:T(8,128)S(1)} %get-tuple-element.35, f32[128,128,128]{2,0,1:T(8,128)} %fusion.64, f32[128,128,128]{2,0,1:T(8,128)} %fusion.52, f32[128,128,128]{2,0,1:T(8,128)} %fusion.54, ...), kind=kOutput, calls=%fused_computation.30 | convolution fusion | flops 558104576 | bytes 37879808 | tf_op jit(solution)/shard_map/pa,rab->rpb/dot_general | solution.py:64
  201.0 3.4 fusion.2
  204.5 3.5 fusion.3
  208.0 6.2 %maximum_bitcast_fusion = bf16[128,2,128,128]{0,3,2,1:T(8,128)(2,1)} fusion(bf16[1,128,128,128]{2,3,1,0:T(8,128)(2,1)} %fusion.3, bf16[1,128,128,128]{2,3,1,0:T(8,128)(2,1)S(1)} %copy-done.7), kind=kLoop, calls=%fused_computation.18 | loop fusion | flops 4194304 | bytes 16777216 | tf_op jit(solution)/shard_map/transpose | solution.py:15
  214.2 6.2 %fusion.148 = (bf16[128,2,64,128]{0,3,2,1:T(8,128)(2,1)}, bf16[128,2,64,128]{0,3,2,1:T(8,128)(2,1)}) fusion(bf16[128,2,128,128]{0,3,2,1:T(8,128)(2,1)} %maximum_bitcast_fusion), kind=kLoop, calls=%fused_computation.183 | loop fusion | bytes 16777216 | tf_op jit(solution)/shard_map/split | solution.py:33
  220.4 6.6 %copy.31 = bf16[128,2,64,128]{3,2,1,0:T(8,128)(2,1)} copy(bf16[128,2,64,128]{0,3,2,1:T(8,128)(2,1)} %get-tuple-element.21) | data formatting | bytes 8388608 | tf_op jit(solution)/shard_map/split | solution.py:33
  226.9 20.6 %all-to-all-start.1 = ((bf16[128,2,64,128]{3,2,1,0:T(8,128)(2,1)}), bf16[128,2,64,128]{3,2,1,0:T(8,128)(2,1)}, u32[]{:S(2)}, u32[]{:S(2)}) async-start(bf16[128,2,64,128]{3,2,1,0:T(8,128)(2,1)} %copy.31), calls=%async_computation.1 | async-start | bytes 8388608 | tf_op jit(solution)/shard_map/all_to_all | solution.py:35
  247.5 6.5 %copy.32 = bf16[128,2,64,128]{3,2,1,0:T(8,128)(2,1)} copy(bf16[128,2,64,128]{0,3,2,1:T(8,128)(2,1)} %get-tuple-element.22) | data formatting | bytes 8388608 | tf_op jit(solution)/shard_map/split | solution.py:33
  254.0 42.8 %all-to-all-done.1 = bf16[128,2,64,128]{3,2,1,0:T(8,128)(2,1)} async-done(((bf16[128,2,64,128]{3,2,1,0:T(8,128)(2,1)}), bf16[128,2,64,128]{3,2,1,0:T(8,128)(2,1)}, u32[]{:S(2)}, u32[]{:S(2)}) %all-to-all-start.1) | async-done | bytes 4194336 | tf_op jit(solution)/shard_map/all_to_all | solution.py:35
  296.8 9.8 %all-to-all-start.2 = ((bf16[128,2,64,128]{3,2,1,0:T(8,128)(2,1)}), bf16[128,2,64,128]{3,2,1,0:T(8,128)(2,1)}, u32[]{:S(2)}, u32[]{:S(2)}) async-start(bf16[128,2,64,128]{3,2,1,0:T(8,128)(2,1)} %copy.32), calls=%async_computation.2 | async-start | bytes 8388608 | tf_op jit(solution)/shard_map/all_to_all | solution.py:35
  315.3 6.9 %copy.33 = bf16[128,2,64,128]{3,0,2,1:T(8,128)(2,1)} copy(bf16[128,2,64,128]{3,2,1,0:T(8,128)(2,1)} %all-to-all-done.1) | data formatting | bytes 8388608 | tf_op jit(solution)/shard_map/all_to_all | solution.py:35
  322.2 33.5 %all-to-all-done.2 = bf16[128,2,64,128]{3,2,1,0:T(8,128)(2,1)} async-done(((bf16[128,2,64,128]{3,2,1,0:T(8,128)(2,1)}), bf16[128,2,64,128]{3,2,1,0:T(8,128)(2,1)}, u32[]{:S(2)}, u32[]{:S(2)}) %all-to-all-start.2) | async-done | bytes 4194336 | tf_op jit(solution)/shard_map/all_to_all | solution.py:35
  355.7 6.9 %copy.34 = bf16[128,2,64,128]{3,0,2,1:T(8,128)(2,1)} copy(bf16[128,2,64,128]{3,2,1,0:T(8,128)(2,1)} %all-to-all-done.2) | data formatting | bytes 8388608 | tf_op jit(solution)/shard_map/all_to_all | solution.py:35
  362.6 7.5 %maximum_bitcast_fusion.1 = bf16[2,128,128,128]{3,1,2,0:T(8,128)(2,1)} fusion(bf16[128,2,64,128]{3,0,2,1:T(8,128)(2,1)} %copy.34, bf16[128,2,64,128]{3,0,2,1:T(8,128)(2,1)} %copy.33), kind=kLoop, calls=%fused_computation.19 | loop fusion | flops 4194304 | bytes 16777216 | tf_op jit(solution)/shard_map/transpose | solution.py:26
  370.0 3.8 fusion.5
  374.7 4.7 fusion.6
  379.4 4.7 fusion.8
  384.1 9.0 %subtract_convert_fusion.1 = (bf16[128,128,128]{2,0,1:T(8,128)(2,1)S(1)}, bf16[128,128,128]{2,0,1:T(8,128)(2,1)S(1)}) fusion(f32[128,128]{0,1:T(8,128)S(1)} %copy.36, f32[128,128]{0,1:T(8,128)S(1)} %copy.35, f32[128,128,128]{2,0,1:T(8,128)S(1)} %fusion.5, f32[128,128,128]{2,0,1:T(8,128)} %fusion.6, f32[128,128,128]{2,0,1:T(8,128)} %fusion.8, ...), kind=kOutput, calls=%fused_computation.25 | convolution fusion | flops 558104576 | bytes 37879808 | tf_op jit(solution)/shard_map/pg,gic->pic/dot_general | solution.py:67
  393.1 6.7 %fusion.9 = f32[128,128,128]{2,0,1:T(8,128)} fusion(bf16[128,128,128]{2,0,1:T(8,128)(2,1)S(1)} %get-tuple-element.9), kind=kOutput, calls=%fused_computation.42 | convolution fusion | flops 537133056 | bytes 12582912 | tf_op jit(solution)/shard_map/qi,pic->qpc/dot_general | solution.py:67
  399.8 3.4 fusion.11
  403.2 7.2 %add_convert_fusion = bf16[128,128,128]{2,0,1:T(8,128)(2,1)S(1)} fusion(f32[128,128,128]{2,0,1:T(8,128)} %fusion.9, bf16[128,128,128]{2,0,1:T(8,128)(2,1)S(1)} %get-tuple-element.8), kind=kOutput, calls=%fused_computation.22 | convolution fusion | flops 541327360 | bytes 16777216 | tf_op jit(solution)/shard_map/qi,pic->qpc/dot_general | solution.py:69
  410.4 2.9 copy.42
  413.4 3.8 subtract_convert_fusion
  417.2 2.7 copy.39
  423.3 3.5 collective-permute-start.1
  426.7 1.9 collective-permute-start.2
  435.3 10.5 %collective-permute-done = bf16[2,1024,128]{2,1,0:T(8,128)(2,1)} collective-permute-done((bf16[2,1024,128]{2,1,0:T(8,128)(2,1)S(1)}, bf16[2,1024,128]{2,1,0:T(8,128)(2,1)}, u32[]{:S(2)}, u32[]{:S(2)}) %collective-permute-start) | collective-permute-done | bytes 524320 | tf_op jit(solution)/shard_map/ppermute | solution.py:42
  449.2 6.1 %collective-permute-done.3 = bf16[2,1024,128]{2,1,0:T(8,128)(2,1)} collective-permute-done((bf16[2,1024,128]{2,1,0:T(8,128)(2,1)S(1)}, bf16[2,1024,128]{2,1,0:T(8,128)(2,1)}, u32[]{:S(2)}, u32[]{:S(2)}) %collective-permute-start.3) | collective-permute-done | bytes 524320 | tf_op jit(solution)/shard_map/ppermute | solution.py:42
  456.5 2.4 fusion.30
  458.9 2.1 copy-done.8
  461.0 18.3 %collective-permute-start.5 = (bf16[2,1024,128]{2,1,0:T(8,128)(2,1)}, bf16[2,1024,128]{2,1,0:T(8,128)(2,1)S(1)}, u32[]{:S(2)}, u32[]{:S(2)}) collective-permute-start(bf16[2,1024,128]{2,1,0:T(8,128)(2,1)} %get-tuple-element.20), channel_id=1, source_target_pairs={{2,0},{3,1},{4,2},{5,3},{6,4},{7,5},{8,6},{9,7},{10,8},{11,9},{12,... | collective-permute-start | bytes 1572872 | tf_op jit(solution)/shard_map/ppermute | solution.py:42
  479.4 3.7 collective-permute-start.7
  483.4 2.4 multiply_multiply_fusion
  488.1 2.1 constant_dynamic-update-slice_fusion.3
  490.2 2.6 collective-permute-done.5
  493.7 11.5 %collective-permute-done.6 = bf16[2,1024,128]{2,1,0:T(8,128)(2,1)S(1)} collective-permute-done((bf16[2,1024,128]{2,1,0:T(8,128)(2,1)S(1)}, bf16[2,1024,128]{2,1,0:T(8,128)(2,1)S(1)}, u32[]{:S(2)}, u32[]{:S(2)}) %collective-permute-start.6) | collective-permute-done | bytes 524320 | tf_op jit(solution)/shard_map/ppermute | solution.py:42
  506.1 10.3 %collective-permute-done.7 = bf16[2,1024,128]{2,1,0:T(8,128)(2,1)S(1)} collective-permute-done((bf16[2,1024,128]{2,1,0:T(8,128)(2,1)S(1)}, bf16[2,1024,128]{2,1,0:T(8,128)(2,1)S(1)}, u32[]{:S(2)}, u32[]{:S(2)}) %collective-permute-start.7) | collective-permute-done | bytes 524320 | tf_op jit(solution)/shard_map/ppermute | solution.py:42
  517.3 6.9 %fusion.4 = bf16[1,2,1024,1024]{3,2,1,0:T(8,128)(2,1)} fusion(f32[1024,1024]{1,0:T(8,128)S(1)} %copy-done.6, bf16[2,1024,1152]{2,1,0:T(8,128)(2,1)} %constant_dynamic-update-slice_fusion, s32[]{:T(128)S(6)} %select_n.211), kind=kLoop, calls=%fused_computation.34 | loop fusion | flops 6291456 | bytes 12582916 | tf_op jit(solution)/shard_map/broadcast_in_dim | solution.py:130
  (49 shorter events, 18.9 us)
Async XLA Ops:
  16.4 120.1 %all-to-all-start = ((bf16[2,1024,2048]{2,0,1:T(2,128)(2,1)}), bf16[2,1024,2048]{2,0,1:T(2,128)(2,1)}, u32[]{:S(2)}, u32[]{:S(2)}) async-start(bf16[2,1024,2048]{2,0,1:T(2,128)(2,1)} %copy.29), calls=%async_computation | async-start | bytes 16777216 | tf_op jit(solution)/shard_map/all_to_all | solution.py:95
  161.3 7.1 %copy-start.2 = (bf16[128,128,128]{2,1,0:T(8,128)(2,1)S(1)}, bf16[128,128,128]{2,1,0:T(8,128)(2,1)}, u32[]{:S(2)}) copy-start(bf16[128,128,128]{2,1,0:T(8,128)(2,1)} %squeeze.11) | copy-start | bytes 12582916
  180.4 7.1 %copy-start.1 = (bf16[128,128,128]{2,1,0:T(8,128)(2,1)S(1)}, bf16[128,128,128]{2,1,0:T(8,128)(2,1)}, u32[]{:S(2)}) copy-start(bf16[128,128,128]{2,1,0:T(8,128)(2,1)} %squeeze.10) | copy-start | bytes 12582916
  204.5 3.5 copy-start.7
  226.9 69.8 %all-to-all-start.1 = ((bf16[128,2,64,128]{3,2,1,0:T(8,128)(2,1)}), bf16[128,2,64,128]{3,2,1,0:T(8,128)(2,1)}, u32[]{:S(2)}, u32[]{:S(2)}) async-start(bf16[128,2,64,128]{3,2,1,0:T(8,128)(2,1)} %copy.31), calls=%async_computation.1 | async-start | bytes 8388608 | tf_op jit(solution)/shard_map/all_to_all | solution.py:35
  254.0 53.0 %copy-start.9 = (s32[128]{0:T(128)S(1)}, s32[128]{0:T(128)}, u32[]{:S(2)}) copy-start(s32[128]{0:T(128)} %param.6) | copy-start | bytes 1540
  254.0 53.0 %copy-start.10 = (s32[128]{0:T(128)S(1)}, s32[128]{0:T(128)}, u32[]{:S(2)}) copy-start(s32[128]{0:T(128)} %param.7) | copy-start | bytes 1540
  254.0 53.0 %copy-start.11 = (s32[128]{0:T(128)S(1)}, s32[128]{0:T(128)}, u32[]{:S(2)}) copy-start(s32[128]{0:T(128)} %param.5) | copy-start | bytes 1540
  296.8 58.9 %all-to-all-start.2 = ((bf16[128,2,64,128]{3,2,1,0:T(8,128)(2,1)}), bf16[128,2,64,128]{3,2,1,0:T(8,128)(2,1)}, u32[]{:S(2)}, u32[]{:S(2)}) async-start(bf16[128,2,64,128]{3,2,1,0:T(8,128)(2,1)} %copy.32), calls=%async_computation.2 | async-start | bytes 8388608 | tf_op jit(solution)/shard_map/all_to_all | solution.py:35
  370.0 4.6 copy-start
  413.4 6.5 %copy-start.3 = (bf16[128,128,128]{2,1,0:T(8,128)(2,1)}, bf16[128,128,128]{2,1,0:T(8,128)(2,1)S(1)}, u32[]{:S(2)}) copy-start(bf16[128,128,128]{2,1,0:T(8,128)(2,1)S(1)} %copy.42) | copy-start | bytes 12582916
  419.9 2.0 copy-start.5
  421.9 23.8 %collective-permute-start = (bf16[2,1024,128]{2,1,0:T(8,128)(2,1)S(1)}, bf16[2,1024,128]{2,1,0:T(8,128)(2,1)}, u32[]{:S(2)}, u32[]{:S(2)}) collective-permute-start(bf16[2,1024,128]{2,1,0:T(8,128)(2,1)S(1)} %get-tuple-element.13), channel_id=1, source_target_pairs={{124,0},{125,1},{126,2},{127,3},{0,4},{1,5},{2,6},{3,7},{4,8},{5,9... | collective-permute-start | bytes 1572872 | tf_op jit(solution)/shard_map/ppermute | solution.py:42
  423.3 23.6 %collective-permute-start.1 = (bf16[2,1024,128]{2,1,0:T(8,128)(2,1)S(1)}, bf16[2,1024,128]{2,1,0:T(8,128)(2,1)}, u32[]{:S(2)}, u32[]{:S(2)}) collective-permute-start(bf16[2,1024,128]{2,1,0:T(8,128)(2,1)S(1)} %get-tuple-element.14), channel_id=1, source_target_pairs={{125,0},{126,1},{127,2},{0,3},{1,4},{2,5},{3,6},{4,7},{5,8},{6,9},... | collective-permute-start | bytes 1572872 | tf_op jit(solution)/shard_map/ppermute | solution.py:42
  426.7 21.4 %collective-permute-start.2 = (bf16[2,1024,128]{2,1,0:T(8,128)(2,1)S(1)}, bf16[2,1024,128]{2,1,0:T(8,128)(2,1)}, u32[]{:S(2)}, u32[]{:S(2)}) collective-permute-start(bf16[2,1024,128]{2,1,0:T(8,128)(2,1)S(1)} %get-tuple-element.15), channel_id=1, source_target_pairs={{126,0},{127,1},{0,2},{1,3},{2,4},{3,5},{4,6},{5,7},{6,8},{7,9},{8... | collective-permute-start | bytes 1572872 | tf_op jit(solution)/shard_map/ppermute | solution.py:42
  428.6 26.7 %collective-permute-start.3 = (bf16[2,1024,128]{2,1,0:T(8,128)(2,1)S(1)}, bf16[2,1024,128]{2,1,0:T(8,128)(2,1)}, u32[]{:S(2)}, u32[]{:S(2)}) collective-permute-start(bf16[2,1024,128]{2,1,0:T(8,128)(2,1)S(1)} %get-tuple-element.16), channel_id=1, source_target_pairs={{127,0},{0,1},{1,2},{2,3},{3,4},{4,5},{5,6},{6,7},{7,8},{8,9},{9,1... | collective-permute-start | bytes 1572872 | tf_op jit(solution)/shard_map/ppermute | solution.py:42
  434.5 22.0 %copy-start.4 = (bf16[128,128,128]{2,1,0:T(8,128)(2,1)S(1)}, bf16[128,128,128]{2,1,0:T(8,128)(2,1)}, u32[]{:S(2)}) copy-start(bf16[128,128,128]{2,1,0:T(8,128)(2,1)} %copy-done.3) | copy-start | bytes 12582916
  434.5 53.6 %collective-permute-start.4 = (bf16[2,1024,128]{2,1,0:T(8,128)(2,1)S(1)}, bf16[2,1024,128]{2,1,0:T(8,128)(2,1)}, u32[]{:S(2)}, u32[]{:S(2)}) collective-permute-start(bf16[2,1024,128]{2,1,0:T(8,128)(2,1)S(1)} %get-tuple-element.17), channel_id=1, source_target_pairs={{1,0},{2,1},{3,2},{4,3},{5,4},{6,5},{7,6},{8,7},{9,8},{10,9},{11,1... | collective-permute-start | bytes 1572872 | tf_op jit(solution)/shard_map/ppermute | solution.py:42
  458.9 2.1 copy-start.8
  461.0 31.8 %collective-permute-start.5 = (bf16[2,1024,128]{2,1,0:T(8,128)(2,1)}, bf16[2,1024,128]{2,1,0:T(8,128)(2,1)S(1)}, u32[]{:S(2)}, u32[]{:S(2)}) collective-permute-start(bf16[2,1024,128]{2,1,0:T(8,128)(2,1)} %get-tuple-element.20), channel_id=1, source_target_pairs={{2,0},{3,1},{4,2},{5,3},{6,4},{7,5},{8,6},{9,7},{10,8},{11,9},{12,... | collective-permute-start | bytes 1572872 | tf_op jit(solution)/shard_map/ppermute | solution.py:42
  479.4 37.0 %collective-permute-start.7 = (bf16[2,1024,128]{2,1,0:T(8,128)(2,1)S(1)}, bf16[2,1024,128]{2,1,0:T(8,128)(2,1)S(1)}, u32[]{:S(2)}, u32[]{:S(2)}) collective-permute-start(bf16[2,1024,128]{2,1,0:T(8,128)(2,1)S(1)} %get-tuple-element.12), channel_id=1, source_target_pairs={{4,0},{5,1},{6,2},{7,3},{8,4},{9,5},{10,6},{11,7},{12,8},{13,9},{1... | collective-permute-start | bytes 1572872 | tf_op jit(solution)/shard_map/ppermute | solution.py:42
  483.1 22.1 %collective-permute-start.6 = (bf16[2,1024,128]{2,1,0:T(8,128)(2,1)S(1)}, bf16[2,1024,128]{2,1,0:T(8,128)(2,1)S(1)}, u32[]{:S(2)}, u32[]{:S(2)}) collective-permute-start(bf16[2,1024,128]{2,1,0:T(8,128)(2,1)S(1)} %get-tuple-element.18), channel_id=1, source_target_pairs={{3,0},{4,1},{5,2},{6,3},{7,4},{8,5},{9,6},{10,7},{11,8},{12,9},{13... | collective-permute-start | bytes 1572872 | tf_op jit(solution)/shard_map/ppermute | solution.py:42
  488.1 29.2 %copy-start.6 = (f32[1024,1024]{1,0:T(8,128)S(1)}, f32[1024,1024]{1,0:T(8,128)}, u32[]{:S(2)}) copy-start(f32[1024,1024]{1,0:T(8,128)} %multiply_multiply_fusion) | copy-start | bytes 12582916
where the time goes:
time: 534 us; the launch traced here: 525 us
  waiting for transfers between devices  232 us (43%)
  local copies, waits for them, and re-layouts  103 us (19%)
  matrix products  82.6 us (15%)
  starting transfers between devices  66 us (12%)
  other arithmetic  27 us (5%)
  between operations  14.5 us (3%)
    all_to_all x1, waiting for transfers between devices, shards(): lax.all_to_all(sky_image, 'col', split_axis=1, concat_axis=2, tiled=True)  115 us
    all_to_all x2, waiting for transfers between devices, cut_exchange(): lax.all_to_all(share, axis, split_axis=0, concat_axis=0, tiled=True)  76.2 us
    ppermute x8, waiting for transfers between devices, shifted(): return lax.ppermute(block, axis, route)  41 us
    ppermute x8, starting transfers between devices, shifted(): return lax.ppermute(block, axis, route)  30.5 us
    all_to_all x2, starting transfers between devices, cut_exchange(): lax.all_to_all(share, axis, split_axis=0, concat_axis=0, tiled=True)  30.4 us
    unnamed x32, local copies, waits for them, and re-layouts  28.9 us
    dot_general x4, matrix products, complex_mix(): jnp.einsum(formula, tables[0], values[1], preferred_element_type=jnp.floa...  21.9 us
    dot_general x4, matrix products, complex_mix(): jnp.einsum(formula, tables[1], values[0], preferred_element_type=jnp.floa...  21.6 us
  transfers between devices with their start and end apart: 11, of which 8 were waited for; matrix products, arithmetic and copies ran while one was open for 6% of the time, Pallas kernels for 0%

commit v1 on v0

--- a/solution.py
+++ b/solution.py
@@ -7,6 +7,13 @@
 N = 16384
 FS = 1024
 SPLIT = 128
+
+
+def exchange_blocks(x, axis, split, join):
+    size = lax.axis_size(axis)
+    blocks = jnp.stack(jnp.split(x, size, axis=split), axis=0)
+    blocks = lax.all_to_all(blocks, axis, split_axis=0, concat_axis=0)
+    return jnp.concatenate(blocks, axis=join)
 
 
 def split_up(shard, dim, devices):
@@ -92,7 +99,7 @@
 
 
 def shards(sky_image, facet_rows, facet_offsets, facet_owner):
-    strip_rows = lax.all_to_all(sky_image, "col", split_axis=1, concat_axis=2, tiled=True)
+    strip_rows = exchange_blocks(sky_image, "col", 1, 2)
     rows_done = rows_pass(strip_rows)
     row_devices = lax.axis_size("row")
     col_devices = lax.axis_size("col")

time: 534 us -> 550 us (1.030)
  local copies, waits for them, and re-layouts: 103 us -> 114 us
    unnamed x32 -> x52, local copies, waits for them, and re-layouts: 28.9 us -> 38.3 us
    dot_general x4, matrix products: 21.9 us -> 29.9 us  [complex_mix(): jnp.einsum(formula, tables[0], values[1], preferred_element_type=jnp.floa...]
    dot_general x4, matrix products: 20.6 us -> 14.7 us  [complex_mix(): jnp.einsum(formula, tables[0], values[0], preferred_element_type=jnp.floa...]
    split x0 -> x1, local copies, waits for them, and re-layouts: none -> 5.6 us  [exchange_blocks(): blocks = jnp.stack(jnp.split(x, size, axis=split), axis=0)]
  transfers between devices with their start and end apart: 11 -> 11, of which waited for: 8 -> 8; matrix products, arithmetic and copies ran while one was open for 6% -> 5% of each run, Pallas kernels for 0% -> 0%
where the time goes in v1:
time: 550 us; the launch traced here: 540 us
  waiting for transfers between devices  232 us (42%)
  local copies, waits for them, and re-layouts  114 us (21%)
  matrix products  85.1 us (15%)
  starting transfers between devices  65.9 us (12%)
  other arithmetic  28.6 us (5%)
  between operations  14.1 us (3%)
    all_to_all x1, waiting for transfers between devices, exchange_blocks(): blocks = lax.all_to_all(blocks, axis, split_axis=0, concat_axis=0)  114 us
    all_to_all x2, waiting for transfers between devices, cut_exchange(): lax.all_to_all(share, axis, split_axis=0, concat_axis=0, tiled=True)  76.8 us
    ppermute x8, waiting for transfers between devices, shifted(): return lax.ppermute(block, axis, route)  41.2 us
    unnamed x52, local copies, waits for them, and re-layouts  38.3 us
    ppermute x8, starting transfers between devices, shifted(): return lax.ppermute(block, axis, route)  30.4 us
    all_to_all x2, starting transfers between devices, cut_exchange(): lax.all_to_all(share, axis, split_axis=0, concat_axis=0, tiled=True)  30.4 us
    dot_general x4, matrix products, complex_mix(): jnp.einsum(formula, tables[0], values[1], preferred_element_type=jnp.floa...  29.9 us
    dot_general x4, matrix products, complex_mix(): jnp.einsum(formula, tables[1], values[0], preferred_element_type=jnp.floa...  22.7 us
  transfers between devices with their start and end apart: 11, of which 8 were waited for; matrix products, arithmetic and copies ran while one was open for 5% of the time, Pallas kernels for 0%

profile of v1, /device:TPU:21, one launch (start us, length us, event | category | flops | bytes accessed | tf_op | source)
XLA Modules:
  0.0 540.4 jit_solution(2547450172804181989)
XLA Ops:
  0.0 5.6 %fusion.152 = (bf16[2,128,2048]{2,1,0:T(8,128)(2,1)S(1)}, bf16[2,128,2048]{2,1,0:T(8,128)(2,1)S(1)}, bf16[2,128,2048]{2,1,0:T(8,128)(2,1)S(1)}, bf16[2,128,2048]...) fusion(bf16[2,1024,2048]{2,1,0:T(8,128)(2,1)} %param.4), kind=kLoop, calls=%fused_computation.197 | loop fusion | bytes 16777216 | tf_op jit(solution)/shard_map/split | solution.py:14
  12.4 2.3 copy.88
  17.0 2.3 copy.90
  21.9 2.4 bitcast_dynamic-update-slice_fusion.6
  32.0 5.1 all-to-all-start
  37.8 114.4 %all-to-all-done = bf16[8,2,128,2048]{2,3,1,0:T(8,128)(2,1)} async-done(((bf16[8,2,128,2048]{2,3,1,0:T(8,128)(2,1)}), bf16[8,2,128,2048]{2,3,1,0:T(8,128)(2,1)}, u32[]{:S(2)}, u32[]{:S(2)}) %all-to-all-start) | async-done | bytes 8388640 | tf_op jit(solution)/shard_map/all_to_all | solution.py:15
  152.2 7.5 %copy.107 = bf16[8,2,128,2048]{2,3,0,1:T(8,128)(2,1)} copy(bf16[8,2,128,2048]{2,3,1,0:T(8,128)(2,1)} %all-to-all-done) | data formatting | bytes 16777216 | tf_op jit(solution)/shard_map/all_to_all | solution.py:15
  159.7 5.8 %fusion.151 = (bf16[1,128,8,2048]{1,3,2,0:T(8,128)(2,1)}, bf16[1,128,8,2048]{1,3,2,0:T(8,128)(2,1)}) fusion(bf16[2,128,8,2048]{1,3,2,0:T(8,128)(2,1)} %bitcast.121), kind=kLoop, calls=%fused_computation.196 | loop fusion | bytes 16777216 | tf_op jit(solution)/shard_map/slice | solution.py:95
  165.5 7.3 %copy.60 = bf16[128,128,128]{1,2,0:T(8,128)(2,1)} copy(bf16[128,128,128]{0,2,1:T(8,128)(2,1)} %bitcast.123) | data formatting | bytes 8388608 | tf_op jit(solution)/shard_map/squeeze | solution.py:95
  172.8 7.1 %fusion.54 = f32[128,128,128]{2,1,0:T(8,128)} fusion(bf16[128,128,128]{1,2,0:T(8,128)(2,1)} %copy.60), kind=kOutput, calls=%fused_computation.107 | convolution fusion | flops 537133056 | bytes 12582912 | tf_op jit(solution)/shard_map/pa,rab->rpb/dot_general | solution.py:76
  179.9 4.7 fusion.68
  184.6 7.2 %copy.61 = bf16[128,128,128]{1,2,0:T(8,128)(2,1)} copy(bf16[128,128,128]{0,2,1:T(8,128)(2,1)} %bitcast.122) | data formatting | bytes 8388608 | tf_op jit(solution)/shard_map/squeeze | solution.py:95
  191.8 7.1 %fusion.56 = f32[128,128,128]{2,1,0:T(8,128)} fusion(bf16[128,128,128]{1,2,0:T(8,128)(2,1)} %copy.61), kind=kOutput, calls=%fused_computation.108 | convolution fusion | flops 537133056 | bytes 12582912 | tf_op jit(solution)/shard_map/pa,rab->rpb/dot_general | solution.py:73
  198.9 12.6 %fusion.1 = (bf16[128,128,128]{1,2,0:T(8,128)(2,1)S(1)}, bf16[128,128,128]{1,2,0:T(8,128)(2,1)}) fusion(f32[128,128]{0,1:T(8,128)S(1)} %copy.65, f32[128,128]{0,1:T(8,128)S(1)} %copy.62, f32[128,128,128]{2,1,0:T(8,128)} %fusion.54, f32[128,128,128]{2,1,0:T(8,128)} %fusion.68, f32[128,128,128]{2,1,0:T(8,128)} %fusion.56, bf16[128,128,128]{1,2,0:T(8,128)(2,1)S(1)} %copy-done.1), kind=kOutput, calls=%fused_computation.23 | convolution fusion | flops 558104576 | bytes 37879808 | tf_op jit(solution)/shard_map/pa,rab->rpb/dot_general | solution.py:74
  215.2 3.5 fusion.4
  218.7 3.6 fusion.5
  222.3 7.5 %maximum_bitcast_fusion = bf16[128,2,128,128]{0,3,2,1:T(8,128)(2,1)} fusion(bf16[1,128,128,128]{2,3,1,0:T(8,128)(2,1)} %fusion.5, bf16[1,128,128,128]{2,3,1,0:T(8,128)(2,1)} %fusion.4), kind=kLoop, calls=%fused_computation.18 | loop fusion | flops 4194304 | bytes 16777216 | tf_op jit(solution)/shard_map/transpose | solution.py:22
  229.9 6.2 %fusion.150 = (bf16[128,2,64,128]{0,3,2,1:T(8,128)(2,1)}, bf16[128,2,64,128]{0,3,2,1:T(8,128)(2,1)}) fusion(bf16[128,2,128,128]{0,3,2,1:T(8,128)(2,1)} %maximum_bitcast_fusion), kind=kLoop, calls=%fused_computation.195 | loop fusion | bytes 16777216 | tf_op jit(solution)/shard_map/split | solution.py:40
  236.0 6.6 %copy.70 = bf16[128,2,64,128]{3,2,1,0:T(8,128)(2,1)} copy(bf16[128,2,64,128]{0,3,2,1:T(8,128)(2,1)} %get-tuple-element.21) | data formatting | bytes 8388608 | tf_op jit(solution)/shard_map/split | solution.py:40
  242.6 20.5 %all-to-all-start.1 = ((bf16[128,2,64,128]{3,2,1,0:T(8,128)(2,1)}), bf16[128,2,64,128]{3,2,1,0:T(8,128)(2,1)}, u32[]{:S(2)}, u32[]{:S(2)}) async-start(bf16[128,2,64,128]{3,2,1,0:T(8,128)(2,1)} %copy.70), calls=%async_computation.1 | async-start | bytes 8388608 | tf_op jit(solution)/shard_map/all_to_all | solution.py:42
  263.1 6.5 %copy.71 = bf16[128,2,64,128]{3,2,1,0:T(8,128)(2,1)} copy(bf16[128,2,64,128]{0,3,2,1:T(8,128)(2,1)} %get-tuple-element.22) | data formatting | bytes 8388608 | tf_op jit(solution)/shard_map/split | solution.py:40
  269.6 42.8 %all-to-all-done.1 = bf16[128,2,64,128]{3,2,1,0:T(8,128)(2,1)} async-done(((bf16[128,2,64,128]{3,2,1,0:T(8,128)(2,1)}), bf16[128,2,64,128]{3,2,1,0:T(8,128)(2,1)}, u32[]{:S(2)}, u32[]{:S(2)}) %all-to-all-start.1) | async-done | bytes 4194336 | tf_op jit(solution)/shard_map/all_to_all | solution.py:42
  312.4 9.8 %all-to-all-start.2 = ((bf16[128,2,64,128]{3,2,1,0:T(8,128)(2,1)}), bf16[128,2,64,128]{3,2,1,0:T(8,128)(2,1)}, u32[]{:S(2)}, u32[]{:S(2)}) async-start(bf16[128,2,64,128]{3,2,1,0:T(8,128)(2,1)} %copy.71), calls=%async_computation.2 | async-start | bytes 8388608 | tf_op jit(solution)/shard_map/all_to_all | solution.py:42
  330.4 6.9 %copy.72 = bf16[128,2,64,128]{3,0,2,1:T(8,128)(2,1)} copy(bf16[128,2,64,128]{3,2,1,0:T(8,128)(2,1)} %all-to-all-done.1) | data formatting | bytes 8388608 | tf_op jit(solution)/shard_map/all_to_all | solution.py:42
  337.3 34.0 %all-to-all-done.2 = bf16[128,2,64,128]{3,2,1,0:T(8,128)(2,1)} async-done(((bf16[128,2,64,128]{3,2,1,0:T(8,128)(2,1)}), bf16[128,2,64,128]{3,2,1,0:T(8,128)(2,1)}, u32[]{:S(2)}, u32[]{:S(2)}) %all-to-all-start.2) | async-done | bytes 4194336 | tf_op jit(solution)/shard_map/all_to_all | solution.py:42
  371.3 6.9 %copy.73 = bf16[128,2,64,128]{3,0,2,1:T(8,128)(2,1)} copy(bf16[128,2,64,128]{3,2,1,0:T(8,128)(2,1)} %all-to-all-done.2) | data formatting | bytes 8388608 | tf_op jit(solution)/shard_map/all_to_all | solution.py:42
  378.2 7.5 %maximum_bitcast_fusion.1 = bf16[2,128,128,128]{3,1,2,0:T(8,128)(2,1)} fusion(bf16[128,2,64,128]{3,0,2,1:T(8,128)(2,1)} %copy.73, bf16[128,2,64,128]{3,0,2,1:T(8,128)(2,1)} %copy.72), kind=kLoop, calls=%fused_computation.19 | loop fusion | flops 4194304 | bytes 16777216 | tf_op jit(solution)/shard_map/transpose | solution.py:33
  385.6 3.8 fusion.10
  390.3 4.7 fusion.7
  395.0 4.7 fusion.8
  399.7 9.1 %subtract_convert_fusion.1 = (bf16[128,128,128]{2,0,1:T(8,128)(2,1)S(1)}, bf16[128,128,128]{2,0,1:T(8,128)(2,1)S(1)}) fusion(f32[128,128]{0,1:T(8,128)S(1)} %copy.65, f32[128,128]{0,1:T(8,128)S(1)} %copy.62, f32[128,128,128]{2,0,1:T(8,128)} %fusion.7, f32[128,128,128]{2,0,1:T(8,128)} %fusion.8, f32[128,128,128]{2,0,1:T(8,128)S(1)} %fusion.10, ...), kind=kOutput, calls=%fused_computation.33 | convolution fusion | flops 558104576 | bytes 37879808 | tf_op jit(solution)/shard_map/pg,gic->pic/dot_general | solution.py:74
  408.8 6.7 %fusion.11 = f32[128,128,128]{2,0,1:T(8,128)} fusion(bf16[128,128,128]{2,0,1:T(8,128)(2,1)S(1)} %get-tuple-element.9), kind=kOutput, calls=%fused_computation.46 | convolution fusion | flops 537133056 | bytes 12582912 | tf_op jit(solution)/shard_map/qi,pic->qpc/dot_general | solution.py:74
  415.5 3.4 fusion.13
  418.9 7.2 %add_convert_fusion = bf16[128,128,128]{2,0,1:T(8,128)(2,1)S(1)} fusion(f32[128,128,128]{2,0,1:T(8,128)} %fusion.11, bf16[128,128,128]{2,0,1:T(8,128)(2,1)S(1)} %get-tuple-element.8), kind=kOutput, calls=%fused_computation.30 | convolution fusion | flops 541327360 | bytes 16777216 | tf_op jit(solution)/shard_map/qi,pic->qpc/dot_general | solution.py:76
  426.1 2.9 copy.81
  429.1 3.8 subtract_convert_fusion
  432.9 2.7 copy.78
  439.0 3.4 collective-permute-start.1
  450.7 10.8 %collective-permute-done = bf16[2,1024,128]{2,1,0:T(8,128)(2,1)} collective-permute-done((bf16[2,1024,128]{2,1,0:T(8,128)(2,1)S(1)}, bf16[2,1024,128]{2,1,0:T(8,128)(2,1)}, u32[]{:S(2)}, u32[]{:S(2)}) %collective-permute-start) | collective-permute-done | bytes 524320 | tf_op jit(solution)/shard_map/ppermute | solution.py:49
  465.0 6.1 %collective-permute-done.3 = bf16[2,1024,128]{2,1,0:T(8,128)(2,1)} collective-permute-done((bf16[2,1024,128]{2,1,0:T(8,128)(2,1)S(1)}, bf16[2,1024,128]{2,1,0:T(8,128)(2,1)}, u32[]{:S(2)}, u32[]{:S(2)}) %collective-permute-start.3) | collective-permute-done | bytes 524320 | tf_op jit(solution)/shard_map/ppermute | solution.py:49
  472.2 2.5 fusion.32
  476.8 18.2 %collective-permute-start.5 = (bf16[2,1024,128]{2,1,0:T(8,128)(2,1)}, bf16[2,1024,128]{2,1,0:T(8,128)(2,1)S(1)}, u32[]{:S(2)}, u32[]{:S(2)}) collective-permute-start(bf16[2,1024,128]{2,1,0:T(8,128)(2,1)} %get-tuple-element.20), channel_id=1, source_target_pairs={{2,0},{3,1},{4,2},{5,3},{6,4},{7,5},{8,6},{9,7},{10,8},{11,9},{12,... | collective-permute-start | bytes 1572872 | tf_op jit(solution)/shard_map/ppermute | solution.py:49
  495.1 3.7 collective-permute-start.7
  499.0 2.4 multiply_multiply_fusion
  506.0 2.5 collective-permute-done.5
  509.4 11.5 %collective-permute-done.6 = bf16[2,1024,128]{2,1,0:T(8,128)(2,1)S(1)} collective-permute-done((bf16[2,1024,128]{2,1,0:T(8,128)(2,1)S(1)}, bf16[2,1024,128]{2,1,0:T(8,128)(2,1)S(1)}, u32[]{:S(2)}, u32[]{:S(2)}) %collective-permute-start.6) | collective-permute-done | bytes 524320 | tf_op jit(solution)/shard_map/ppermute | solution.py:49
  521.9 10.2 %collective-permute-done.7 = bf16[2,1024,128]{2,1,0:T(8,128)(2,1)S(1)} collective-permute-done((bf16[2,1024,128]{2,1,0:T(8,128)(2,1)S(1)}, bf16[2,1024,128]{2,1,0:T(8,128)(2,1)S(1)}, u32[]{:S(2)}, u32[]{:S(2)}) %collective-permute-start.7) | collective-permute-done | bytes 524320 | tf_op jit(solution)/shard_map/ppermute | solution.py:49
  533.0 6.9 %fusion.6 = bf16[1,2,1024,1024]{3,2,1,0:T(8,128)(2,1)} fusion(f32[1024,1024]{1,0:T(8,128)S(1)} %copy-done.7, bf16[2,1024,1152]{2,1,0:T(8,128)(2,1)} %constant_dynamic-update-slice_fusion, s32[]{:T(128)S(6)} %select_n.211), kind=kLoop, calls=%fused_computation.38 | loop fusion | flops 6291456 | bytes 12582916 | tf_op jit(solution)/shard_map/broadcast_in_dim | solution.py:137
  (72 shorter events, 45.3 us)
Async XLA Ops:
  21.9 4.7 copy-start.11
  21.9 5.7 %copy-start.10 = (bf16[2,128,2048]{1,2,0:T(8,128)(2,1)S(1)}, bf16[2,128,2048]{1,2,0:T(8,128)(2,1)}, u32[]{:S(2)}) copy-start(bf16[2,128,2048]{1,2,0:T(8,128)(2,1)} %copy.90) | copy-start | bytes 3145732
  21.9 6.8 %copy-start.9 = (bf16[2,128,2048]{1,2,0:T(8,128)(2,1)S(1)}, bf16[2,128,2048]{1,2,0:T(8,128)(2,1)}, u32[]{:S(2)}) copy-start(bf16[2,128,2048]{1,2,0:T(8,128)(2,1)} %copy.91) | copy-start | bytes 3145732
  32.0 120.2 %all-to-all-start = ((bf16[8,2,128,2048]{2,3,1,0:T(8,128)(2,1)}), bf16[8,2,128,2048]{2,3,1,0:T(8,128)(2,1)}, u32[]{:S(2)}, u32[]{:S(2)}) async-start(bf16[8,2,128,2048]{2,3,1,0:T(8,128)(2,1)} %bitcast_dynamic-update-slice_fusion), calls=%async_computation | async-start | bytes 16777216 | tf_op jit(solution)/shard_map/all_to_all | solution.py:15
  172.8 7.1 %copy-start.2 = (bf16[128,128,128]{1,2,0:T(8,128)(2,1)S(1)}, bf16[128,128,128]{1,2,0:T(8,128)(2,1)}, u32[]{:S(2)}) copy-start(bf16[128,128,128]{1,2,0:T(8,128)(2,1)} %copy.60) | copy-start | bytes 12582916
  191.8 7.1 %copy-start.1 = (bf16[128,128,128]{1,2,0:T(8,128)(2,1)S(1)}, bf16[128,128,128]{1,2,0:T(8,128)(2,1)}, u32[]{:S(2)}) copy-start(bf16[128,128,128]{1,2,0:T(8,128)(2,1)} %copy.61) | copy-start | bytes 12582916
  211.5 2.2 copy-start.6
  242.6 69.8 %all-to-all-start.1 = ((bf16[128,2,64,128]{3,2,1,0:T(8,128)(2,1)}), bf16[128,2,64,128]{3,2,1,0:T(8,128)(2,1)}, u32[]{:S(2)}, u32[]{:S(2)}) async-start(bf16[128,2,64,128]{3,2,1,0:T(8,128)(2,1)} %copy.70), calls=%async_computation.1 | async-start | bytes 8388608 | tf_op jit(solution)/shard_map/all_to_all | solution.py:42
  269.6 52.8 %copy-start.12 = (s32[128]{0:T(128)S(1)}, s32[128]{0:T(128)}, u32[]{:S(2)}) copy-start(s32[128]{0:T(128)} %param.6) | copy-start | bytes 1540
  269.6 52.8 %copy-start.13 = (s32[128]{0:T(128)S(1)}, s32[128]{0:T(128)}, u32[]{:S(2)}) copy-start(s32[128]{0:T(128)} %param.7) | copy-start | bytes 1540
  269.6 52.8 %copy-start.14 = (s32[128]{0:T(128)S(1)}, s32[128]{0:T(128)}, u32[]{:S(2)}) copy-start(s32[128]{0:T(128)} %param.5) | copy-start | bytes 1540
  312.4 58.9 %all-to-all-start.2 = ((bf16[128,2,64,128]{3,2,1,0:T(8,128)(2,1)}), bf16[128,2,64,128]{3,2,1,0:T(8,128)(2,1)}, u32[]{:S(2)}, u32[]{:S(2)}) async-start(bf16[128,2,64,128]{3,2,1,0:T(8,128)(2,1)} %copy.71), calls=%async_computation.2 | async-start | bytes 8388608 | tf_op jit(solution)/shard_map/all_to_all | solution.py:42
  385.6 4.6 copy-start
  429.1 6.5 %copy-start.3 = (bf16[128,128,128]{2,1,0:T(8,128)(2,1)}, bf16[128,128,128]{2,1,0:T(8,128)(2,1)S(1)}, u32[]{:S(2)}) copy-start(bf16[128,128,128]{2,1,0:T(8,128)(2,1)S(1)} %copy.81) | copy-start | bytes 12582916
  435.6 2.0 copy-start.5
  437.6 23.9 %collective-permute-start = (bf16[2,1024,128]{2,1,0:T(8,128)(2,1)S(1)}, bf16[2,1024,128]{2,1,0:T(8,128)(2,1)}, u32[]{:S(2)}, u32[]{:S(2)}) collective-permute-start(bf16[2,1024,128]{2,1,0:T(8,128)(2,1)S(1)} %get-tuple-element.13), channel_id=1, source_target_pairs={{124,0},{125,1},{126,2},{127,3},{0,4},{1,5},{2,6},{3,7},{4,8},{5,9... | collective-permute-start | bytes 1572872 | tf_op jit(solution)/shard_map/ppermute | solution.py:49
  439.0 23.6 %collective-permute-start.1 = (bf16[2,1024,128]{2,1,0:T(8,128)(2,1)S(1)}, bf16[2,1024,128]{2,1,0:T(8,128)(2,1)}, u32[]{:S(2)}, u32[]{:S(2)}) collective-permute-start(bf16[2,1024,128]{2,1,0:T(8,128)(2,1)S(1)} %get-tuple-element.14), channel_id=1, source_target_pairs={{125,0},{126,1},{127,2},{0,3},{1,4},{2,5},{3,6},{4,7},{5,8},{6,9},... | collective-permute-start | bytes 1572872 | tf_op jit(solution)/shard_map/ppermute | solution.py:49
  442.4 21.4 %collective-permute-start.2 = (bf16[2,1024,128]{2,1,0:T(8,128)(2,1)S(1)}, bf16[2,1024,128]{2,1,0:T(8,128)(2,1)}, u32[]{:S(2)}, u32[]{:S(2)}) collective-permute-start(bf16[2,1024,128]{2,1,0:T(8,128)(2,1)S(1)} %get-tuple-element.15), channel_id=1, source_target_pairs={{126,0},{127,1},{0,2},{1,3},{2,4},{3,5},{4,6},{5,7},{6,8},{7,9},{8... | collective-permute-start | bytes 1572872 | tf_op jit(solution)/shard_map/ppermute | solution.py:49
  444.3 26.7 %collective-permute-start.3 = (bf16[2,1024,128]{2,1,0:T(8,128)(2,1)S(1)}, bf16[2,1024,128]{2,1,0:T(8,128)(2,1)}, u32[]{:S(2)}, u32[]{:S(2)}) collective-permute-start(bf16[2,1024,128]{2,1,0:T(8,128)(2,1)S(1)} %get-tuple-element.16), channel_id=1, source_target_pairs={{127,0},{0,1},{1,2},{2,3},{3,4},{4,5},{5,6},{6,7},{7,8},{8,9},{9,1... | collective-permute-start | bytes 1572872 | tf_op jit(solution)/shard_map/ppermute | solution.py:49
  449.9 22.3 %copy-start.4 = (bf16[128,128,128]{2,1,0:T(8,128)(2,1)S(1)}, bf16[128,128,128]{2,1,0:T(8,128)(2,1)}, u32[]{:S(2)}) copy-start(bf16[128,128,128]{2,1,0:T(8,128)(2,1)} %copy-done.3) | copy-start | bytes 12582916
  449.9 54.0 %collective-permute-start.4 = (bf16[2,1024,128]{2,1,0:T(8,128)(2,1)S(1)}, bf16[2,1024,128]{2,1,0:T(8,128)(2,1)}, u32[]{:S(2)}, u32[]{:S(2)}) collective-permute-start(bf16[2,1024,128]{2,1,0:T(8,128)(2,1)S(1)} %get-tuple-element.17), channel_id=1, source_target_pairs={{1,0},{2,1},{3,2},{4,3},{5,4},{6,5},{7,6},{8,7},{9,8},{10,9},{11,1... | collective-permute-start | bytes 1572872 | tf_op jit(solution)/shard_map/ppermute | solution.py:49
  474.7 2.1 copy-start.8
  476.8 31.7 %collective-permute-start.5 = (bf16[2,1024,128]{2,1,0:T(8,128)(2,1)}, bf16[2,1024,128]{2,1,0:T(8,128)(2,1)S(1)}, u32[]{:S(2)}, u32[]{:S(2)}) collective-permute-start(bf16[2,1024,128]{2,1,0:T(8,128)(2,1)} %get-tuple-element.20), channel_id=1, source_target_pairs={{2,0},{3,1},{4,2},{5,3},{6,4},{7,5},{8,6},{9,7},{10,8},{11,9},{12,... | collective-permute-start | bytes 1572872 | tf_op jit(solution)/shard_map/ppermute | solution.py:49
  495.1 37.0 %collective-permute-start.7 = (bf16[2,1024,128]{2,1,0:T(8,128)(2,1)S(1)}, bf16[2,1024,128]{2,1,0:T(8,128)(2,1)S(1)}, u32[]{:S(2)}, u32[]{:S(2)}) collective-permute-start(bf16[2,1024,128]{2,1,0:T(8,128)(2,1)S(1)} %get-tuple-element.12), channel_id=1, source_target_pairs={{4,0},{5,1},{6,2},{7,3},{8,4},{9,5},{10,6},{11,7},{12,8},{13,9},{1... | collective-permute-start | bytes 1572872 | tf_op jit(solution)/shard_map/ppermute | solution.py:49
  498.8 22.1 %collective-permute-start.6 = (bf16[2,1024,128]{2,1,0:T(8,128)(2,1)S(1)}, bf16[2,1024,128]{2,1,0:T(8,128)(2,1)S(1)}, u32[]{:S(2)}, u32[]{:S(2)}) collective-permute-start(bf16[2,1024,128]{2,1,0:T(8,128)(2,1)S(1)} %get-tuple-element.18), channel_id=1, source_target_pairs={{3,0},{4,1},{5,2},{6,3},{7,4},{8,5},{9,6},{10,7},{11,8},{12,9},{13... | collective-permute-start | bytes 1572872 | tf_op jit(solution)/shard_map/ppermute | solution.py:49
  503.9 29.1 %copy-start.7 = (f32[1024,1024]{1,0:T(8,128)S(1)}, f32[1024,1024]{1,0:T(8,128)}, u32[]{:S(2)}) copy-start(f32[1024,1024]{1,0:T(8,128)} %multiply_multiply_fusion) | copy-start | bytes 12582916
